TPU v7x, 256 devices: a whole 4x4x8 slice. The times are simulated.
256 devices in a mesh: dp: 4 (over x), seq: 64 (over z, y, core).
Axes of the slice: x: 4, y: 4, z: 8, core: 2. Of those that a mesh axis runs over, the one named last changes fastest.
Arguments:
- streams: bfloat16 [3, 4, 8192, 4096], P(None, 'dp', 'seq'), may hold values from -6 to 6
- short_filter: float32 [3, 3, 4096], P(None, None, 'dp'), may hold values from -3.5 to 3.5
- decay_rate: float32 [2, 4096], P(None, 'dp'), may hold values from 1.2207031e-06 to 0.05
- pole_angle: float32 [2, 4096], P(None, 'dp'), may hold values from -3.140625 to 3.140625
- residue_re: float32 [2, 4096], P(None, 'dp'), may hold values from -6 to 6
- residue_im: float32 [2, 4096], P(None, 'dp'), may hold values from -6 to 6
- skip_gain: float32 [4096], P('dp'), may hold values from -6 to 6
- doc_starts: int32 [4, 8], P('dp'), may hold values from 0 to 8191, as said below
Outputs:
- mixed: bfloat16 [4, 8192, 4096], P('dp', 'seq')
Inputs may be any that keep to these rules, and one draw needn't show every extreme that they name: `doc_starts`: each row starts with 0 and rises strictly; the last document of every sequence is one position long.
All inputs are finite; a program needn't handle non-finite values.
Results may differ from a plain program's by a relative error of at most 0.0045.
Values may be sent and summed in bfloat16 or wider, within the bound.
A program may use at most 128 MiB of HBM per device.

v0:
```python
import jax
import jax.numpy as jnp
from jax import lax
from jax.sharding import PartitionSpec as P

block_len = 32


def from_behind(x, axis, by):
    count = lax.axis_size(axis)
    pairs = [(i, i + by) for i in range(count) if 0 <= i + by < count]
    return lax.ppermute(x, axis, pairs)


def prefix_2(part, axis, combine, identity):
    place = lax.axis_index(axis)
    gathered = jax.tree.map(lambda a: lax.all_gather(a, axis), part)
    state = jax.tree.map(lambda a, e: jnp.zeros_like(a) + jnp.asarray(e, a.dtype), part, identity)

    def one(turn, state):
        return combine(
            state, jax.tree.map(lambda a: lax.dynamic_index_in_dim(a, turn, 0, False), gathered)
        )

    return lax.fori_loop(0, place, one, state)


def pole_power(decay, rotation, powers):
    magnitude = jnp.exp(-decay * powers)
    return (magnitude * jnp.cos(rotation * powers), magnitude * jnp.sin(rotation * powers))


def segment_of(positions, starts):
    return jnp.sum((positions[..., None] >= starts).astype(jnp.int32), axis=-1) - 1


def local(
    streams, short_filter, decay_rate, pole_angle, residue_re, residue_im, skip_gain, doc_starts
):
    short_filter, decay_rate, pole_angle, residue_re, residue_im, skip_gain = (
        lax.all_gather(short_filter, "dp", axis=2, tiled=True),
        lax.all_gather(decay_rate, "dp", axis=1, tiled=True),
        lax.all_gather(pole_angle, "dp", axis=1, tiled=True),
        lax.all_gather(residue_re, "dp", axis=1, tiled=True),
        lax.all_gather(residue_im, "dp", axis=1, tiled=True),
        lax.all_gather(skip_gain, "dp", axis=0, tiled=True),
    )
    tok_rows = streams.shape[2]
    channels = streams.shape[3]
    modes = decay_rate.shape[0]
    my_index = lax.axis_index("seq")
    offset = my_index * tok_rows
    starts = doc_starts[0]
    rim_rows = streams[:, :, tok_rows - 2 :, :]
    before = from_behind(rim_rows, "seq", 1)
    extended = jnp.concatenate([before, streams], axis=2)[:, 0]
    filtered = (
        short_filter[0][:, None, :] * extended[:, 2:]
        + short_filter[1][:, None, :] * extended[:, 1:-1]
        + short_filter[2][:, None, :] * extended[:, :-2]
    )
    product = filtered[0] * filtered[1]
    out_gate = filtered[2]
    positions = offset + jnp.arange(tok_rows, dtype=jnp.int32)
    seg_ids = segment_of(positions, starts)
    seg_before = segment_of(offset - 1 + jnp.zeros((1,), jnp.int32), starts)[0]
    nblocks = tok_rows // block_len
    local_steps = jnp.arange(block_len, dtype=jnp.float32)[:, None, None]
    fwd_re, fwd_im = pole_power(decay_rate, pole_angle, local_steps)
    back_re, back_im = pole_power(-decay_rate, -pole_angle, local_steps)
    blocked = product.reshape(nblocks, block_len, 1, channels)
    lifted = jnp.concatenate([blocked * back_re, blocked * back_im], axis=2)
    lifted = lifted.reshape(nblocks, block_len, 2 * modes * channels)
    seg_blocks = seg_ids.reshape(nblocks, block_len)
    causal = jnp.arange(block_len)[:, None] >= jnp.arange(block_len)[None, :]
    within = (causal[None] & (seg_blocks[:, :, None] == seg_blocks[:, None, :])).astype(jnp.float32)
    summed = jnp.einsum("bts,bsk->btk", within, lifted, precision=lax.Precision.HIGHEST)
    summed = summed.reshape(nblocks, block_len, 2 * modes, channels)
    sum_re = summed[:, :, :modes]
    sum_im = summed[:, :, modes:]
    state_re = fwd_re * sum_re - fwd_im * sum_im
    state_im = fwd_re * sum_im + fwd_im * sum_re
    step_re, step_im = pole_power(decay_rate, pole_angle, jnp.float32(block_len))
    entry_seg = jnp.concatenate([seg_before[None], seg_blocks[:-1, -1]])
    keeps_last = (seg_blocks[:, -1] == entry_seg).astype(jnp.float32)

    def advance(running, inputs):
        run_re, run_im = running
        last_re, last_im, kept_now = inputs
        next_re = last_re + kept_now * (step_re * run_re - step_im * run_im)
        next_im = last_im + kept_now * (step_re * run_im + step_im * run_re)
        return ((next_re, next_im), (run_re, run_im))

    zero_state = jnp.zeros((modes, channels), jnp.float32)
    (end_re, end_im), (entry_re, entry_im) = lax.scan(
        advance, (zero_state, zero_state), (state_re[:, -1], state_im[:, -1], keeps_last)
    )
    lead_re, lead_im = pole_power(decay_rate, pole_angle, local_steps + 1.0)
    joined = (seg_blocks == entry_seg[:, None]).astype(jnp.float32)[:, :, None, None]
    state_re = state_re + joined * (lead_re * entry_re[:, None] - lead_im * entry_im[:, None])
    state_im = state_im + joined * (lead_re * entry_im[:, None] + lead_im * entry_re[:, None])
    whole_re, whole_im = pole_power(decay_rate, pole_angle, jnp.float32(tok_rows))
    keep_all = (seg_ids[-1] == seg_before).astype(jnp.float32)

    def combine(earlier, latter):
        early_are, early_aim, early_sre, early_sim = earlier
        late_are, late_aim, late_sre, late_sim = latter
        return (
            late_are * early_are - late_aim * early_aim,
            late_are * early_aim + late_aim * early_are,
            late_sre + late_are * early_sre - late_aim * early_sim,
            late_sim + late_are * early_sim + late_aim * early_sre,
        )

    unit_state = jnp.ones_like(end_re)
    prefix = prefix_2(
        (keep_all * whole_re, keep_all * whole_im, end_re, end_im),
        "seq",
        combine,
        (unit_state, zero_state, zero_state, zero_state),
    )
    inflow_re = prefix[2]
    inflow_im = prefix[3]
    all_steps = (
        jnp.arange(tok_rows, dtype=jnp.float32).reshape(nblocks, block_len)[:, :, None, None] + 1.0
    )
    enter_re, enter_im = pole_power(decay_rate, pole_angle, all_steps)
    reach = (seg_blocks == seg_before).astype(jnp.float32)[:, :, None, None]
    state_re = state_re + reach * (enter_re * inflow_re - enter_im * inflow_im)
    state_im = state_im + reach * (enter_re * inflow_im + enter_im * inflow_re)
    norm_factor = jnp.sqrt(-jnp.expm1(-2.0 * decay_rate))
    long_part = jnp.sum(norm_factor * (residue_re * state_re - residue_im * state_im), axis=2)
    long_part = long_part.reshape(tok_rows, channels)
    response = skip_gain * product + long_part
    return (out_gate * response).astype(jnp.bfloat16)[None]


def solution(mesh):
    placed = (
        P(None, "dp", "seq", None),
        P(None, None, "dp"),
        P(None, "dp"),
        P(None, "dp"),
        P(None, "dp"),
        P(None, "dp"),
        P("dp"),
        P("dp", None),
    )
    return jax.shard_map(
        local, mesh=mesh, in_specs=placed, out_specs=P("dp", "seq", None), check_vma=False
    )
```

profile of v0, /device:TPU:249, one launch (start us, length us, event | category | flops | bytes accessed | tf_op | source)
XLA Modules:
  0.0 430.3 jit_solution(6064338715635104115)
XLA Ops:
  6.5 1.3 fusion.14
  10.5 9.6 %all_gather.46 = f32[2,4096]{1,0:T(2,128)S(1)} all-gather(f32[2,1024]{1,0:T(2,128)} %param.15), channel_id=1, replica_groups=mesh['dp'=4,'seq'=64] {'dp'}, dimensions={1}, use_global_device_ids=true | all-gather | bytes 40960 | tf_op jit(solution)/shard_map/all_gather | solution.py:43
  20.1 9.2 %all_gather.44 = f32[2,4096]{1,0:T(2,128)S(1)} all-gather(f32[2,1024]{1,0:T(2,128)} %param.14), channel_id=1, replica_groups=mesh['dp'=4,'seq'=64] {'dp'}, dimensions={1}, use_global_device_ids=true | all-gather | bytes 40960 | tf_op jit(solution)/shard_map/all_gather | solution.py:42
  29.3 1.7 multiply_bitcast_fusion
  31.0 1.0 slice.69
  32.0 1.3 collective-permute-start
  33.8 16.3 %cosine_multiply_fusion = (f32[32,2,4096]{2,1,0:T(2,128)}, f32[32,2,4096]{2,1,0:T(2,128)}) fusion(f32[2,4096]{1,0:T(2,128)S(1)} %get-tuple-element.233, f32[2,4096]{1,0:T(2,128)S(1)} %all_gather.44), kind=kLoop, calls=%fused_computation.37 | loop fusion | flops 1048576 | bytes 2162688 | tf_op jit(solution)/shard_map/mul | solution.py:30
  50.2 9.8 %all_gather.42 = f32[3,3,4096]{2,1,0:T(4,128)S(1)} all-gather(f32[3,3,1024]{2,1,0:T(4,128)} %param.13), channel_id=1, replica_groups=mesh['dp'=4,'seq'=64] {'dp'}, dimensions={2}, use_global_device_ids=true | all-gather | bytes 184320 | tf_op jit(solution)/shard_map/all_gather | solution.py:41
  60.0 8.6 %fusion.6 = (f32[32,2,4096]{2,0,1:T(8,128)S(1)}, f32[32,2,4096]{2,0,1:T(8,128)S(1)}, f32[32,2,4096]{2,0,1:T(8,128)}, f32[32,2,4096]{2,0,1:T(8,128)}) fusion(f32[32]{0:T(128)S(1)} %iota_add_fusion, f32[2,4096]{1,0:T(2,128)S(1)} %all_gather.46, f32[2,4096]{1,0:T(2,128)S(1)} %get-tuple-element.234), kind=kLoop, calls=%fused_computation.32 | loop fusion | flops 2097152 | bytes 4259968 | tf_op jit(solution)/shard_map/mul | solution.py:30
  68.7 2.7 maximum_bitcast_fusion
  71.4 2.1 multiply_add_fusion
  73.8 1.7 copy-done.4
  75.6 1.1 copy-done.5
  76.7 3.9 broadcast_multiply_fusion.1
  80.5 9.7 %pad_maximum_fusion = f32[4,32,4,4096]{3,2,1,0:T(4,128)} fusion(f32[4,32,2,4096]{3,2,1,0:T(2,128)} %get-tuple-element.218, f32[4,32,2,4096]{3,2,1,0:T(2,128)S(1)} %get-tuple-element.217), kind=kLoop, calls=%fused_computation.14 | loop fusion | flops 2097152 | bytes 16777216 | tf_op jit(solution)/shard_map/concatenate | solution.py:72
  90.3 11.0 %reshape.158 = f32[4,32,16384]{2,1,0:T(8,128)} reshape(f32[4,32,4,4096]{3,2,1,0:T(4,128)} %pad_maximum_fusion) | data formatting | bytes 16777216 | tf_op jit(solution)/shard_map/reshape | solution.py:73
  101.3 10.8 %fusion.8 = f32[4,32,16384]{2,1,0:T(8,128)} fusion(f32[4,32,16384]{2,1,0:T(8,128)} %reshape.158, s32[4,32]{1,0:T(4,128)S(1)} %sub.35, pred[32,32]{1,0:T(8,128)(4,1)S(1)} %iota_compare_fusion), kind=kOutput, calls=%fused_computation.48 | convolution fusion | flops 805314560 | bytes 16778752 | tf_op jit(solution)/shard_map/bts,bsk->btk/dot_general | solution.py:77
  112.1 10.8 %reshape.159 = f32[4,32,4,4096]{3,2,1,0:T(4,128)} reshape(f32[4,32,16384]{2,1,0:T(8,128)} %fusion.8) | data formatting | bytes 16777216 | tf_op jit(solution)/shard_map/reshape | solution.py:78
  122.9 11.1 %fusion.15 = (f32[4,32,2,4096]{3,2,1,0:T(2,128)S(1)}, f32[4,32,2,4096]{3,2,1,0:T(2,128)}) fusion(f32[4,32,4,4096]{3,2,1,0:T(4,128)} %reshape.159), kind=kLoop, calls=%fused_computation.75 | loop fusion | bytes 16777216 | tf_op jit(solution)/shard_map/slice | solution.py:79
  134.0 7.8 %multiply_subtract_fusion = (f32[4,32,2,4096]{3,1,2,0:T(8,128)S(1)}, f32[4,32,2,4096]{3,1,2,0:T(8,128)S(1)}) fusion(f32[4,32,2,4096]{3,2,1,0:T(2,128)} %get-tuple-element.216, f32[4,32,2,4096]{3,2,1,0:T(2,128)S(1)} %get-tuple-element.215, f32[32,2,4096]{2,0,1:T(8,128)S(1)} %copy-done.3, f32[32,2,4096]{2,0,1:T(8,128)} %get-tuple-element.225), kind=kLoop, calls=%fused_computation.22 | loop fusion | flops 6291456 | bytes 18874368 | tf_op jit(solution)/shard_map/sub | solution.py:81
  141.9 2.0 copy-done.1
  144.0 1.1 copy-done.2
  145.5 7.9 %while.33 = (s32[]{:T(128)}, f32[2,4096]{1,0:T(2,128)S(1)}, f32[2,4096]{1,0:T(2,128)S(1)}, f32[4,2,4096]{2,1,0:T(2,128)S(1)}, f32[4,2,4096]{2,1,0:T(2,128)}, /*i...) while((s32[]{:T(128)}, f32[2,4096]{1,0:T(2,128)S(1)}, ...), condition=%wide.region_3.4_spmd.clone, body=%wide.region_2.3_spmd.clone.sunk | while | flops 114691 | bytes 393876 | solution.py:95
  154.6 9.0 %all_gather.43 = f32[4096]{0:T(1024)S(1)} all-gather(f32[1024]{0:T(1024)S(1)} %copy-done.10), channel_id=1, replica_groups=mesh['dp'=4,'seq'=64] {'dp'}, dimensions={0}, use_global_device_ids=true | all-gather | bytes 20480 | tf_op jit(solution)/shard_map/all_gather | solution.py:46
  163.7 9.6 %all_gather.45 = f32[2,4096]{1,0:T(2,128)S(1)} all-gather(f32[2,1024]{1,0:T(2,128)S(1)} %copy-done.8), channel_id=1, replica_groups=mesh['dp'=4,'seq'=64] {'dp'}, dimensions={1}, use_global_device_ids=true | all-gather | bytes 40960 | tf_op jit(solution)/shard_map/all_gather | solution.py:44
  173.2 9.0 %all_gather.55 = f32[2,4096]{1,0:T(2,128)S(1)} all-gather(f32[2,1024]{1,0:T(2,128)S(1)} %copy-done.9), channel_id=1, replica_groups=mesh['dp'=4,'seq'=64] {'dp'}, dimensions={1}, use_global_device_ids=true | all-gather | bytes 40960 | tf_op jit(solution)/shard_map/all_gather | solution.py:45
  182.4 6.7 %all-gather.17.cloned.1.call-done = f32[64,2,4096]{2,1,0:T(2,128)} async-done(((f32[1,2,4096]{2,1,0:T(2,128)}), f32[64,2,4096]{2,1,0:T(2,128)}) %all-gather.17.cloned.1.call-update) | async-done | bytes 2097168 | tf_op jit(solution)/shard_map/all_gather | solution.py:17
  189.1 77.8 %all-gather.13.cloned.1.call-done = f32[64,2,4096]{2,1,0:T(2,128)} async-done(((f32[1,2,4096]{2,1,0:T(2,128)}), f32[64,2,4096]{2,1,0:T(2,128)}) %all-gather.13.cloned.1.call-update) | async-done | bytes 2097168 | tf_op jit(solution)/shard_map/all_gather | solution.py:17
  266.9 77.6 %all-gather.19.cloned.1.call-done = f32[64,2,4096]{2,1,0:T(2,128)} async-done(((f32[1,2,4096]{2,1,0:T(2,128)}), f32[64,2,4096]{2,1,0:T(2,128)}) %all-gather.19.cloned.1.call-update) | async-done | bytes 2097168 | tf_op jit(solution)/shard_map/all_gather | solution.py:17
  344.5 56.3 %while.32 = (s32[]{:T(128)}, f32[2,4096]{1,0:T(2,128)S(1)}, f32[2,4096]{1,0:T(2,128)S(1)}, s32[]{:T(128)}, f32[64,2,4096]{2,1,0:T(2,128)}, /*index=5*/f32[64,2,4...) while((s32[]{:T(128)}, f32[2,4096]{1,0:T(2,128)S(1)}, ...), condition=%wide.region_5.6_spmd, body=%wide.region_4.5_spmd.sunk | while | flops 65541 | bytes 262291 | solution.py:25
  400.8 21.4 %multiply_reduce_fusion = f32[4,32,4096]{2,1,0:T(8,128)S(1)} fusion(f32[4,32,2,4096]{3,1,2,0:T(8,128)} %copy-done.2, f32[4,32,2,4096]{3,1,2,0:T(8,128)} %copy-done.1, f32[2,4096]{1,0:T(2,128)S(1)} %all_gather.55, f32[2,4096]{1,0:T(2,128)S(1)} %get-tuple-element.135, f32[2,4096]{1,0:T(2,128)S(1)} %get-tuple-element.134, f32[2,4096]{1,0:T(2,128)S(1)} %all_gather.46, ...), kind=kLoop, calls=%fused_computation.20 | loop fusion | flops 29884416 | bytes 13075968 | tf_op jit(solution)/shard_map/reduce_sum | solution.py:132
  422.2 1.6 fusion.5
  (131 shorter events, 66.7 us)
Async XLA Ops:
  6.5 175.8 %all-gather.15.cloned.1.call-start = ((), (), s32[]{:S(2)}) async-start(), calls=%async_computation.1 | async-start | bytes 2129920 | tf_op jit(solution)/shard_map/all_gather | solution.py:17
  31.0 158.1 %all-gather.17.cloned.1.call-start = ((), (), s32[]{:S(2)}) async-start(), calls=%async_computation.2 | async-start | bytes 2129920 | tf_op jit(solution)/shard_map/all_gather | solution.py:17
  32.0 36.7 %collective-permute-start = (bf16[3,1,2,4096]{3,2,0,1:T(2,128)(2,1)S(1)}, bf16[3,1,2,4096]{3,2,0,1:T(2,128)(2,1)S(1)}, u32[]{:S(2)}, u32[]{:S(2)}) collective-permute-start(bf16[3,1,2,4096]{3,2,0,1:T(2,128)(2,1)S(1)} %slice.69), channel_id=1, source_target_pairs={{0,1},{1,2},{2,3},{3,4},{4,5},{5,6},{6,7},{7,8},{8,9},{9,10},{10,1... | collective-permute-start | bytes 147464 | tf_op jit(solution)/shard_map/ppermute | solution.py:12
  33.3 233.5 %all-gather.13.cloned.1.call-start = ((), (), s32[]{:S(2)}) async-start(), calls=%async_computation | async-start | bytes 2129920 | tf_op jit(solution)/shard_map/all_gather | solution.py:17
  73.5 7.0 %copy-start = (f32[3,128,4096]{2,1,0:T(8,128)}, f32[3,128,4096]{2,1,0:T(8,128)S(1)}, u32[]{:S(2)}) copy-start(f32[3,128,4096]{2,1,0:T(8,128)S(1)} %multiply_add_fusion) | copy-start | bytes 18874372
  73.6 2.0 copy-start.4
  73.6 3.1 copy-start.5
  122.9 11.1 %copy-start.3 = (f32[32,2,4096]{2,0,1:T(8,128)S(1)}, f32[32,2,4096]{2,0,1:T(8,128)}, u32[]{:S(2)}) copy-start(f32[32,2,4096]{2,0,1:T(8,128)} %get-tuple-element.224) | copy-start | bytes 3145732
  134.0 20.6 %copy-start.10 = (f32[1024]{0:T(1024)S(1)}, f32[1024]{0:T(1024)}, u32[]{:S(2)}) copy-start(f32[1024]{0:T(1024)} %param.18) | copy-start | bytes 12292
  134.0 29.7 %copy-start.8 = (f32[2,1024]{1,0:T(2,128)S(1)}, f32[2,1024]{1,0:T(2,128)}, u32[]{:S(2)}) copy-start(f32[2,1024]{1,0:T(2,128)} %param.16) | copy-start | bytes 24580
  134.0 39.2 %copy-start.9 = (f32[2,1024]{1,0:T(2,128)S(1)}, f32[2,1024]{1,0:T(2,128)}, u32[]{:S(2)}) copy-start(f32[2,1024]{1,0:T(2,128)} %param.17) | copy-start | bytes 24580
  141.8 2.0 copy-start.1
  141.8 3.3 copy-start.2
  153.4 0.6 copy-start.6
  153.4 0.7 copy-start.7
  154.0 190.4 %all-gather.19.cloned.1.call-start = ((), (), s32[]{:S(2)}) async-start(), calls=%async_computation.3 | async-start | bytes 2129920 | tf_op jit(solution)/shard_map/all_gather | solution.py:17
  400.8 21.4 %slice-start = ((s8[6291456]{0:T(1024)(128)(4,1)}), s8[4194304]{0:T(1024)(128)(4,1)S(1)}, s32[]{:S(2)}) async-start(s8[6291456]{0:T(1024)(128)(4,1)} %bitcast.73), calls=%async_computation.4 | async-start | bytes 8388608
  400.8 21.4 %slice-start.1 = ((s8[6291456]{0:T(1024)(128)(4,1)}), s8[2097152]{0:T(1024)(128)(4,1)S(1)}, s32[]{:S(2)}) async-start(s8[6291456]{0:T(1024)(128)(4,1)} %bitcast.73), calls=%async_computation.5 | async-start | bytes 4194304
Sparse Core Ops, SparseCore 0:
  31.1 80.2 all-gather.14
  114.1 74.9 all-gather.16
  191.9 74.9 all-gather.12
  269.5 74.9 all-gather.18
where the time goes:
time: 436 us; the launch traced here: 430 us
  waiting for transfers between devices  163 us (37%)
  other arithmetic  139 us (32%)
  blocking collectives  56.2 us (13%)
  local copies, waits for them, and re-layouts  44.3 us (10%)
  between operations  14.7 us (3%)
  matrix products  10.8 us (2%)
    all_gather x4, waiting for transfers between devices, prefix_2(): gathered = jax.tree.map(lambda a: lax.all_gather(a, axis), part)  162 us
    add x63, other arithmetic, combine(): late_sim + late_are * early_sim + late_aim * early_sre  54.8 us
    mul x2, other arithmetic, pole_power(): magnitude * jnp.cos(rotation * powers)  24.9 us
    reduce_sum x1, other arithmetic, local(): jnp.sum(norm_factor * (residue_re * state_re - residue_im * state_im), ax...  21.4 us
    slice x1, local copies, waits for them, and re-layouts, local(): sum_re = summed[:, :, :modes]  11.1 us
    reshape x1, local copies, waits for them, and re-layouts, local(): lifted = lifted.reshape(nblocks, block_len, 2 * modes * channels)  11 us
    dot_general x1, matrix products, local(): jnp.einsum('bts,bsk->btk', within, lifted, precision=lax.Precision.HIGHEST)  10.8 us
    reshape x1, local copies, waits for them, and re-layouts, local(): summed = summed.reshape(nblocks, block_len, 2 * modes, channels)  10.8 us
  transfers between devices with their start and end apart: 5, of which 3 were waited for; matrix products, arithmetic and copies ran while one was open for 24% of the time, Pallas kernels for 0%

commit v1 on v0

--- a/solution.py
+++ b/solution.py
@@ -40,7 +40,9 @@
     short_filter, decay_rate, pole_angle, residue_re, residue_im, skip_gain = (
         lax.all_gather(short_filter, "dp", axis=2, tiled=True),
         lax.all_gather(decay_rate, "dp", axis=1, tiled=True),
-        lax.all_gather(pole_angle, "dp", axis=1, tiled=True),
+        jnp.concatenate(
+            lax.all_to_all(jnp.stack([pole_angle] * lax.axis_size("dp")), "dp", 0, 0), axis=1
+        ),
         lax.all_gather(residue_re, "dp", axis=1, tiled=True),
         lax.all_gather(residue_im, "dp", axis=1, tiled=True),
         lax.all_gather(skip_gain, "dp", axis=0, tiled=True),

time: 436 us -> 430 us (0.986)
  blocking collectives: 56.2 us -> 47.2 us
    all_gather x1 -> x0, blocking collectives: 9.58 us -> none  [local(): lax.all_gather(pole_angle, 'dp', axis=1, tiled=True)]
  transfers between devices with their start and end apart: 5 -> 6, of which waited for: 3 -> 3; matrix products, arithmetic and copies ran while one was open for 24% -> 25% of each run, Pallas kernels for 0% -> 0%
where the time goes in v1:
time: 430 us; the launch traced here: 424 us
  waiting for transfers between devices  160 us (37%)
  other arithmetic  139 us (32%)
  blocking collectives  47.2 us (11%)
  local copies, waits for them, and re-layouts  45.6 us (11%)
  between operations  14.6 us (3%)
  matrix products  10.8 us (3%)
  starting transfers between devices  5.43 us (1%)
    all_gather x4, waiting for transfers between devices, prefix_2(): gathered = jax.tree.map(lambda a: lax.all_gather(a, axis), part)  160 us
    add x63, other arithmetic, combine(): late_sim + late_are * early_sim + late_aim * early_sre  54.8 us
    mul x2, other arithmetic, pole_power(): magnitude * jnp.cos(rotation * powers)  24.9 us
    reduce_sum x1, other arithmetic, local(): jnp.sum(norm_factor * (residue_re * state_re - residue_im * state_im), ax...  21.3 us
    slice x1, local copies, waits for them, and re-layouts, local(): sum_re = summed[:, :, :modes]  11 us
    reshape x1, local copies, waits for them, and re-layouts, local(): lifted = lifted.reshape(nblocks, block_len, 2 * modes * channels)  10.9 us
    dot_general x1, matrix products, local(): jnp.einsum('bts,bsk->btk', within, lifted, precision=lax.Precision.HIGHEST)  10.8 us
    reshape x1, local copies, waits for them, and re-layouts, local(): summed = summed.reshape(nblocks, block_len, 2 * modes, channels)  10.8 us
  transfers between devices with their start and end apart: 6, of which 3 were waited for; matrix products, arithmetic and copies ran while one was open for 25% of the time, Pallas kernels for 0%

profile of v1, /device:TPU:249, one launch (start us, length us, event | category | flops | bytes accessed | tf_op | source)
XLA Modules:
  0.0 424.2 jit_solution(8819647179601407285)
XLA Ops:
  6.5 1.3 stack.2
  7.9 4.0 all-to-all-start
  12.6 1.3 fusion.14
  15.8 9.8 %all_gather.41 = f32[2,4096]{1,0:T(2,128)S(1)} all-gather(f32[2,1024]{1,0:T(2,128)} %param.14), channel_id=1, replica_groups=mesh['dp'=4,'seq'=64] {'dp'}, dimensions={1}, use_global_device_ids=true | all-gather | bytes 40960 | tf_op jit(solution)/shard_map/all_gather | solution.py:42
  25.6 1.7 multiply_bitcast_fusion
  28.3 1.3 collective-permute-start
  29.7 9.4 %all_gather.39 = f32[3,3,4096]{2,1,0:T(4,128)S(1)} all-gather(f32[3,3,1024]{2,1,0:T(4,128)} %param.13), channel_id=1, replica_groups=mesh['dp'=4,'seq'=64] {'dp'}, dimensions={2}, use_global_device_ids=true | all-gather | bytes 184320 | tf_op jit(solution)/shard_map/all_gather | solution.py:41
  39.7 8.6 %fusion.6 = (f32[32,2,4096]{2,0,1:T(8,128)S(1)}, f32[32,2,4096]{2,0,1:T(8,128)S(1)}, f32[32,2,4096]{2,0,1:T(8,128)}, f32[32,2,4096]{2,0,1:T(8,128)}) fusion(f32[32]{0:T(128)S(1)} %iota_add_fusion, f32[2,4096]{1,0:T(2,128)S(1)} %bitcast.85, f32[2,4096]{1,0:T(2,128)S(1)} %get-tuple-element.234), kind=kLoop, calls=%fused_computation.32 | loop fusion | flops 2097152 | bytes 4259968 | tf_op jit(solution)/shard_map/mul | solution.py:30
  48.3 16.3 %cosine_multiply_fusion = (f32[32,2,4096]{2,1,0:T(2,128)}, f32[32,2,4096]{2,1,0:T(2,128)}) fusion(f32[2,4096]{1,0:T(2,128)S(1)} %get-tuple-element.233, f32[2,4096]{1,0:T(2,128)S(1)} %all_gather.41), kind=kLoop, calls=%fused_computation.37 | loop fusion | flops 1048576 | bytes 2162688 | tf_op jit(solution)/shard_map/mul | solution.py:30
  64.7 2.7 maximum_bitcast_fusion
  67.4 2.3 multiply_add_fusion
  70.0 1.7 copy-done.4
  71.7 1.1 copy-done.5
  72.8 3.9 broadcast_multiply_fusion.1
  76.7 9.7 %pad_maximum_fusion = f32[4,32,4,4096]{3,2,1,0:T(4,128)} fusion(f32[4,32,2,4096]{3,2,1,0:T(2,128)} %get-tuple-element.218, f32[4,32,2,4096]{3,2,1,0:T(2,128)S(1)} %get-tuple-element.217), kind=kLoop, calls=%fused_computation.14 | loop fusion | flops 2097152 | bytes 16777216 | tf_op jit(solution)/shard_map/concatenate | solution.py:74
  86.4 10.9 %reshape.169 = f32[4,32,16384]{2,1,0:T(8,128)} reshape(f32[4,32,4,4096]{3,2,1,0:T(4,128)} %pad_maximum_fusion) | data formatting | bytes 16777216 | tf_op jit(solution)/shard_map/reshape | solution.py:75
  97.3 10.8 %fusion.8 = f32[4,32,16384]{2,1,0:T(8,128)} fusion(f32[4,32,16384]{2,1,0:T(8,128)} %reshape.169, s32[4,32]{1,0:T(4,128)S(1)} %sub.35, pred[32,32]{1,0:T(8,128)(4,1)S(1)} %iota_compare_fusion), kind=kOutput, calls=%fused_computation.48 | convolution fusion | flops 805314560 | bytes 16778752 | tf_op jit(solution)/shard_map/bts,bsk->btk/dot_general | solution.py:79
  108.1 10.8 %reshape.170 = f32[4,32,4,4096]{3,2,1,0:T(4,128)} reshape(f32[4,32,16384]{2,1,0:T(8,128)} %fusion.8) | data formatting | bytes 16777216 | tf_op jit(solution)/shard_map/reshape | solution.py:80
  119.0 11.0 %fusion.15 = (f32[4,32,2,4096]{3,2,1,0:T(2,128)S(1)}, f32[4,32,2,4096]{3,2,1,0:T(2,128)}) fusion(f32[4,32,4,4096]{3,2,1,0:T(4,128)} %reshape.170), kind=kLoop, calls=%fused_computation.75 | loop fusion | bytes 16777216 | tf_op jit(solution)/shard_map/slice | solution.py:81
  130.0 7.8 %multiply_subtract_fusion = (f32[4,32,2,4096]{3,1,2,0:T(8,128)S(1)}, f32[4,32,2,4096]{3,1,2,0:T(8,128)S(1)}) fusion(f32[4,32,2,4096]{3,2,1,0:T(2,128)} %get-tuple-element.216, f32[4,32,2,4096]{3,2,1,0:T(2,128)S(1)} %get-tuple-element.215, f32[32,2,4096]{2,0,1:T(8,128)S(1)} %copy-done.3, f32[32,2,4096]{2,0,1:T(8,128)} %get-tuple-element.225), kind=kLoop, calls=%fused_computation.22 | loop fusion | flops 6291456 | bytes 18874368 | tf_op jit(solution)/shard_map/sub | solution.py:83
  137.9 2.0 copy-done.1
  140.0 1.1 copy-done.2
  141.5 7.9 %while.33 = (s32[]{:T(128)}, f32[2,4096]{1,0:T(2,128)S(1)}, f32[2,4096]{1,0:T(2,128)S(1)}, f32[4,2,4096]{2,1,0:T(2,128)S(1)}, f32[4,2,4096]{2,1,0:T(2,128)}, /*i...) while((s32[]{:T(128)}, f32[2,4096]{1,0:T(2,128)S(1)}, ...), condition=%wide.region_3.4_spmd.clone, body=%wide.region_2.3_spmd.clone.sunk | while | flops 114691 | bytes 393876 | solution.py:97
  150.7 9.0 %all_gather.40 = f32[4096]{0:T(1024)S(1)} all-gather(f32[1024]{0:T(1024)S(1)} %copy-done.10), channel_id=1, replica_groups=mesh['dp'=4,'seq'=64] {'dp'}, dimensions={0}, use_global_device_ids=true | all-gather | bytes 20480 | tf_op jit(solution)/shard_map/all_gather | solution.py:48
  159.7 9.6 %all_gather.42 = f32[2,4096]{1,0:T(2,128)S(1)} all-gather(f32[2,1024]{1,0:T(2,128)S(1)} %copy-done.8), channel_id=1, replica_groups=mesh['dp'=4,'seq'=64] {'dp'}, dimensions={1}, use_global_device_ids=true | all-gather | bytes 40960 | tf_op jit(solution)/shard_map/all_gather | solution.py:46
  169.3 9.4 %all_gather.51 = f32[2,4096]{1,0:T(2,128)S(1)} all-gather(f32[2,1024]{1,0:T(2,128)S(1)} %copy-done.9), channel_id=1, replica_groups=mesh['dp'=4,'seq'=64] {'dp'}, dimensions={1}, use_global_device_ids=true | all-gather | bytes 40960 | tf_op jit(solution)/shard_map/all_gather | solution.py:47
  178.8 4.3 %all-gather.17.cloned.1.call-done = f32[64,2,4096]{2,1,0:T(2,128)} async-done(((f32[1,2,4096]{2,1,0:T(2,128)}), f32[64,2,4096]{2,1,0:T(2,128)}) %all-gather.17.cloned.1.call-update) | async-done | bytes 2097168 | tf_op jit(solution)/shard_map/all_gather | solution.py:17
  183.1 77.7 %all-gather.13.cloned.1.call-done = f32[64,2,4096]{2,1,0:T(2,128)} async-done(((f32[1,2,4096]{2,1,0:T(2,128)}), f32[64,2,4096]{2,1,0:T(2,128)}) %all-gather.13.cloned.1.call-update) | async-done | bytes 2097168 | tf_op jit(solution)/shard_map/all_gather | solution.py:17
  260.8 77.6 %all-gather.19.cloned.1.call-done = f32[64,2,4096]{2,1,0:T(2,128)} async-done(((f32[1,2,4096]{2,1,0:T(2,128)}), f32[64,2,4096]{2,1,0:T(2,128)}) %all-gather.19.cloned.1.call-update) | async-done | bytes 2097168 | tf_op jit(solution)/shard_map/all_gather | solution.py:17
  338.5 56.2 %while.32 = (s32[]{:T(128)}, f32[2,4096]{1,0:T(2,128)S(1)}, f32[2,4096]{1,0:T(2,128)S(1)}, s32[]{:T(128)}, f32[64,2,4096]{2,1,0:T(2,128)}, /*index=5*/f32[64,2,4...) while((s32[]{:T(128)}, f32[2,4096]{1,0:T(2,128)S(1)}, ...), condition=%wide.region_5.6_spmd, body=%wide.region_4.5_spmd.sunk | while | flops 65541 | bytes 262291 | solution.py:25
  394.7 21.3 %multiply_reduce_fusion = f32[4,32,4096]{2,1,0:T(8,128)S(1)} fusion(f32[4,32,2,4096]{3,1,2,0:T(8,128)} %copy-done.2, f32[4,32,2,4096]{3,1,2,0:T(8,128)} %copy-done.1, f32[2,4096]{1,0:T(2,128)S(1)} %all_gather.51, f32[2,4096]{1,0:T(2,128)S(1)} %get-tuple-element.135, f32[2,4096]{1,0:T(2,128)S(1)} %get-tuple-element.134, f32[2,4096]{1,0:T(2,128)S(1)} %bitcast.86, ...), kind=kLoop, calls=%fused_computation.20 | loop fusion | flops 29884416 | bytes 13075968 | tf_op jit(solution)/shard_map/reduce_sum | solution.py:134
  416.1 1.6 fusion.5
  (133 shorter events, 67.7 us)
Async XLA Ops:
  7.9 17.7 %all-to-all-start = ((f32[4,2,1024]{2,1,0:T(2,128)}), f32[4,2,1024]{2,1,0:T(2,128)S(1)}, u32[]{:S(2)}, u32[]{:S(2)}) async-start(f32[4,2,1024]{2,1,0:T(2,128)} %stack.2), calls=%async_computation | async-start | bytes 65536 | tf_op jit(solution)/shard_map/all_to_all | solution.py:44
  11.9 166.9 %all-gather.15.cloned.1.call-start = ((), (), s32[]{:S(2)}) async-start(), calls=%async_computation.2 | async-start | bytes 2129920 | tf_op jit(solution)/shard_map/all_gather | solution.py:17
  27.3 155.8 %all-gather.17.cloned.1.call-start = ((), (), s32[]{:S(2)}) async-start(), calls=%async_computation.3 | async-start | bytes 2129920 | tf_op jit(solution)/shard_map/all_gather | solution.py:17
  28.3 36.3 %collective-permute-start = (bf16[3,1,2,4096]{3,2,0,1:T(2,128)(2,1)S(1)}, bf16[3,1,2,4096]{3,2,0,1:T(2,128)(2,1)S(1)}, u32[]{:S(2)}, u32[]{:S(2)}) collective-permute-start(bf16[3,1,2,4096]{3,2,0,1:T(2,128)(2,1)S(1)} %slice.69), channel_id=1, source_target_pairs={{0,1},{1,2},{2,3},{3,4},{4,5},{5,6},{6,7},{7,8},{8,9},{9,10},{10,1... | collective-permute-start | bytes 147464 | tf_op jit(solution)/shard_map/ppermute | solution.py:12
  64.6 196.2 %all-gather.13.cloned.1.call-start = ((), (), s32[]{:S(2)}) async-start(), calls=%async_computation.1 | async-start | bytes 2129920 | tf_op jit(solution)/shard_map/all_gather | solution.py:17
  69.7 7.0 %copy-start = (f32[3,128,4096]{2,1,0:T(8,128)}, f32[3,128,4096]{2,1,0:T(8,128)S(1)}, u32[]{:S(2)}) copy-start(f32[3,128,4096]{2,1,0:T(8,128)S(1)} %multiply_add_fusion) | copy-start | bytes 18874372
  69.7 2.0 copy-start.4
  69.7 3.1 copy-start.5
  119.0 11.1 %copy-start.3 = (f32[32,2,4096]{2,0,1:T(8,128)S(1)}, f32[32,2,4096]{2,0,1:T(8,128)}, u32[]{:S(2)}) copy-start(f32[32,2,4096]{2,0,1:T(8,128)} %get-tuple-element.224) | copy-start | bytes 3145732
  130.0 20.6 %copy-start.10 = (f32[1024]{0:T(1024)S(1)}, f32[1024]{0:T(1024)}, u32[]{:S(2)}) copy-start(f32[1024]{0:T(1024)} %param.18) | copy-start | bytes 12292
  130.0 29.7 %copy-start.8 = (f32[2,1024]{1,0:T(2,128)S(1)}, f32[2,1024]{1,0:T(2,128)}, u32[]{:S(2)}) copy-start(f32[2,1024]{1,0:T(2,128)} %param.16) | copy-start | bytes 24580
  130.0 39.3 %copy-start.9 = (f32[2,1024]{1,0:T(2,128)S(1)}, f32[2,1024]{1,0:T(2,128)}, u32[]{:S(2)}) copy-start(f32[2,1024]{1,0:T(2,128)} %param.17) | copy-start | bytes 24580
  137.9 2.0 copy-start.1
  137.9 3.3 copy-start.2
  149.4 0.6 copy-start.6
  149.4 0.7 copy-start.7
  150.1 188.4 %all-gather.19.cloned.1.call-start = ((), (), s32[]{:S(2)}) async-start(), calls=%async_computation.4 | async-start | bytes 2129920 | tf_op jit(solution)/shard_map/all_gather | solution.py:17
  394.7 21.4 %slice-start = ((s8[6291456]{0:T(1024)(128)(4,1)}), s8[4194304]{0:T(1024)(128)(4,1)S(1)}, s32[]{:S(2)}) async-start(s8[6291456]{0:T(1024)(128)(4,1)} %bitcast.76), calls=%async_computation.5 | async-start | bytes 8388608
  394.7 21.4 %slice-start.1 = ((s8[6291456]{0:T(1024)(128)(4,1)}), s8[2097152]{0:T(1024)(128)(4,1)S(1)}, s32[]{:S(2)}) async-start(s8[6291456]{0:T(1024)(128)(4,1)} %bitcast.76), calls=%async_computation.6 | async-start | bytes 4194304
Sparse Core Ops, SparseCore 0:
  27.4 77.8 all-gather.14
  108.1 74.9 all-gather.16
  185.9 74.9 all-gather.12
  263.5 74.9 all-gather.18
